TPU v7x, 32 devices: a whole 2x2x4 slice. The times are simulated.
32 devices in a mesh: gx: 8 (over z, y), gy: 4 (over x, core).
Axes of the slice: x: 2, y: 2, z: 4, core: 2. Of those that a mesh axis runs over, the one named last changes fastest.
Arguments:
- layer_in: bfloat16 [8192, 2048], P('gx', 'gy'), may hold values from -15 to 15
- attn_gain: float32 [2048], replicated, may hold values from 0.25 to 1.75
- q_gain: float32 [128], replicated, may hold values from 0.5 to 5
- k_gain: float32 [128], replicated, may hold values from 0.5 to 5
- w_query: bfloat16 [2048, 2048], P('gx', 'gy'), may hold values from -0.125 to 0.125
- w_key: bfloat16 [2048, 1024], P('gx', 'gy'), may hold values from -0.125 to 0.125
- w_value: bfloat16 [2048, 1024], P('gx', 'gy'), may hold values from -0.125 to 0.125
- w_output: bfloat16 [2048, 2048], P('gy', 'gx'), may hold values from -0.375 to 0.375
- mlp_gain: float32 [2048], replicated, may hold values from 0.25 to 1.75
- w_gate: bfloat16 [2048, 6144], P('gx', 'gy'), may hold values from -0.125 to 0.125
- w_up: bfloat16 [2048, 6144], P('gx', 'gy'), may hold values from -0.125 to 0.125
- w_down: bfloat16 [6144, 2048], P('gy', 'gx'), may hold values from -0.078125 to 0.078125
- out_grad: bfloat16 [8192, 2048], P('gx', 'gy'), may hold values from -6 to 6
Outputs:
- layer_out: bfloat16 [8192, 2048], P('gx', 'gy')
- input_grad: float32 [8192, 2048], P('gx', 'gy')
- attn_gain_grad: float32 [2048], replicated
- q_gain_grad: float32 [128], replicated
- k_gain_grad: float32 [128], replicated
- query_grad: float32 [2048, 2048], P('gx', 'gy')
- key_grad: float32 [2048, 1024], P('gx', 'gy')
- value_grad: float32 [2048, 1024], P('gx', 'gy')
- output_grad: float32 [2048, 2048], P('gy', 'gx')
- mlp_gain_grad: float32 [2048], replicated
- gate_grad: float32 [2048, 6144], P('gx', 'gy')
- up_grad: float32 [2048, 6144], P('gx', 'gy')
- down_grad: float32 [6144, 2048], P('gy', 'gx')
All inputs are finite; a program needn't handle non-finite values.
Results may differ from a plain program's by a relative error of at most 0.02.
The roundings to bfloat16 on the way count: a program that leaves them out, or rounds other values in their place, can miss the bound.
Values may be sent and summed in bfloat16 or wider, within the bound.
No kernel may reach another device: no remote copies, remote signals or barrier semaphores. Data moves between devices by JAX's collectives and lax.ppermute only.
A program may use at most 256 MiB of HBM per device.

v0:
```python
import math
import jax
import jax.numpy as jnp
from jax import lax
from jax.sharding import PartitionSpec as P

D = 2048
HQ = 16
HK = 8
HD = 128
L = 512
epsilon = 1e-06
rope_base = 1000000.0


def rope_tables(length, dim_width):
    half_width = dim_width // 2
    frequency = rope_base ** (-(jnp.arange(half_width, dtype=jnp.float32) * (2.0 / dim_width)))
    angles = jnp.arange(length, dtype=jnp.float32)[:, None] * frequency[None, :]
    angles = jnp.concatenate([angles, angles], axis=1)
    return (jnp.cos(angles), jnp.sin(angles))


def rotate(tensor):
    half_width = tensor.shape[-1] // 2
    return jnp.concatenate([-tensor[..., half_width:], tensor[..., :half_width]], axis=-1)


def rotate_back(tensor):
    half_width = tensor.shape[-1] // 2
    return jnp.concatenate([tensor[..., half_width:], -tensor[..., :half_width]], axis=-1)


def head_norm(tensor, gain_vec):
    factor = lax.rsqrt(jnp.mean(tensor * tensor, axis=-1, keepdims=True) + epsilon)
    return (tensor * factor * gain_vec, factor)


def head_norm_back(upstream, tensor, factor, gain_vec):
    weighted = upstream * gain_vec
    return factor * weighted - tensor * factor**3 * jnp.mean(
        weighted * tensor, axis=-1, keepdims=True
    )


def matmul(left, right):
    return jnp.dot(left, right, preferred_element_type=jnp.float32)


def bein(form, left, right):
    return jnp.einsum(form, left, right, preferred_element_type=jnp.float32)


def causal_scores(query_rot, key_rot):
    inv_scale = 1.0 / math.sqrt(HD)
    scores = bein("sihgc,sjhc->shgij", query_rot, key_rot) * inv_scale
    causal = jnp.arange(L)[:, None] >= jnp.arange(L)[None, :]
    return jnp.where(causal, scores, -1e30)


def embed_share(share, column, total_width):
    return lax.dynamic_update_slice(jnp.zeros((total_width,), jnp.float32), share, (column,))


def on_device(
    layer_in,
    attn_gain,
    q_gain,
    k_gain,
    w_query,
    w_key,
    w_value,
    w_output,
    mlp_gain,
    w_gate,
    w_up,
    w_down,
    out_grad,
):
    row_count = layer_in.shape[0]
    part_width = layer_in.shape[1]
    seq_count = row_count // L
    group_size = HQ // HK
    inv_scale = 1.0 / math.sqrt(HD)
    column = lax.axis_index("gy") * part_width
    full_in, grad_full = (
        lax.all_gather(layer_in, "gy", axis=1, tiled=True),
        lax.all_gather(out_grad, "gy", axis=1, tiled=True),
    )
    in_float = full_in.astype(jnp.float32)
    scale_one = lax.rsqrt(jnp.mean(in_float * in_float, axis=1, keepdims=True) + epsilon)
    normed_one = (in_float * scale_one * attn_gain).astype(jnp.bfloat16)
    query_full, key_full, value_full, output_full = (
        lax.all_gather(w_query, "gx", axis=0, tiled=True),
        lax.all_gather(w_key, "gx", axis=0, tiled=True),
        lax.all_gather(w_value, "gx", axis=0, tiled=True),
        lax.all_gather(w_output, "gx", axis=1, tiled=True),
    )
    query_heads = query_full.shape[1] // HD
    key_heads = key_full.shape[1] // HD
    query_act = matmul(normed_one, query_full).reshape(row_count, query_heads, HD)
    key_act = matmul(normed_one, key_full).reshape(row_count, key_heads, HD)
    values = (
        matmul(normed_one, value_full).astype(jnp.bfloat16).reshape(seq_count, L, key_heads, HD)
    )
    query_normed, query_factor = head_norm(query_act, q_gain)
    key_normed, key_factor = head_norm(key_act, k_gain)
    cosine, sine = rope_tables(L, HD)
    cosine = cosine[None, :, None, :]
    sine = sine[None, :, None, :]
    query_seq = query_normed.reshape(seq_count, L, query_heads, HD)
    key_seq = key_normed.reshape(seq_count, L, key_heads, HD)
    query_rot = (
        (query_seq * cosine + rotate(query_seq) * sine)
        .astype(jnp.bfloat16)
        .reshape(seq_count, L, key_heads, group_size, HD)
    )
    key_rot = (key_seq * cosine + rotate(key_seq) * sine).astype(jnp.bfloat16)
    scores = causal_scores(query_rot, key_rot)
    row_top = jnp.max(scores, axis=-1, keepdims=True)
    log_total = row_top + jnp.log(jnp.sum(jnp.exp(scores - row_top), axis=-1, keepdims=True))
    probs = jnp.exp(scores - log_total).astype(jnp.bfloat16)
    attended = bein("shgij,sjhc->sihgc", probs, values).astype(jnp.bfloat16)
    attended_flat = attended.reshape(row_count, query_heads * HD)
    attn_sum = lax.psum(matmul(attended_flat, output_full), "gy")
    mid_float = in_float + attn_sum
    scale_two = lax.rsqrt(jnp.mean(mid_float * mid_float, axis=1, keepdims=True) + epsilon)
    normed_two = (mid_float * scale_two * mlp_gain).astype(jnp.bfloat16)
    gate_full, up_full, down_full = (
        lax.all_gather(w_gate, "gx", axis=0, tiled=True),
        lax.all_gather(w_up, "gx", axis=0, tiled=True),
        lax.all_gather(w_down, "gx", axis=1, tiled=True),
    )
    gate_act = matmul(normed_two, gate_full)
    up_act = matmul(normed_two, up_full)
    sigmoid_gate = jax.nn.sigmoid(gate_act)
    hidden = (gate_act * sigmoid_gate * up_act).astype(jnp.bfloat16)
    mlp_share = lax.psum_scatter(
        matmul(hidden, down_full).astype(jnp.bfloat16), "gy", scatter_dimension=1, tiled=True
    ).astype(jnp.float32)
    mid_share = lax.dynamic_slice_in_dim(mid_float, column, part_width, 1)
    layer_out = (mid_share + mlp_share).astype(jnp.bfloat16)
    grad_hidden = matmul(grad_full, down_full.T)
    down_term = matmul(hidden.T, grad_full)
    grad_gate = (
        grad_hidden * up_act * sigmoid_gate * (1.0 + gate_act * (1.0 - sigmoid_gate))
    ).astype(jnp.bfloat16)
    grad_up = (grad_hidden * gate_act * sigmoid_gate).astype(jnp.bfloat16)
    gate_term = matmul(normed_two.T, grad_gate)
    up_term = matmul(normed_two.T, grad_up)
    grad_two_part = matmul(grad_gate, gate_full.T) + matmul(grad_up, up_full.T)
    grad_two = lax.psum(grad_two_part, "gy")
    mlp_gain_all = jnp.sum(grad_two * mid_float * scale_two, axis=0)
    mlp_gain_own = lax.dynamic_slice_in_dim(mlp_gain_all, column, part_width, 0)
    grad_mid = (
        grad_full.astype(jnp.float32)
        + scale_two * mlp_gain * grad_two
        - mid_float
        * scale_two**3
        * jnp.mean(mlp_gain * grad_two * mid_float, axis=1, keepdims=True)
    )
    grad_mid_bf = grad_mid.astype(jnp.bfloat16)
    grad_mid_share = lax.dynamic_slice_in_dim(grad_mid, column, part_width, 1)
    gate_grad, up_grad, down_grad = (
        lax.psum_scatter(
            gate_term.astype(jnp.bfloat16), "gx", scatter_dimension=0, tiled=True
        ).astype(jnp.float32),
        lax.psum_scatter(
            up_term.astype(jnp.bfloat16), "gx", scatter_dimension=0, tiled=True
        ).astype(jnp.float32),
        lax.psum_scatter(
            down_term.astype(jnp.bfloat16), "gx", scatter_dimension=1, tiled=True
        ).astype(jnp.float32),
    )
    grad_att = matmul(grad_mid_bf, output_full.T).astype(jnp.bfloat16)
    output_term = matmul(attended_flat.T, grad_mid_bf)
    grad_att_seq = grad_att.reshape(seq_count, L, key_heads, group_size, HD)
    probs_again = jnp.exp(causal_scores(query_rot, key_rot) - log_total)
    probs_bf = probs_again.astype(jnp.bfloat16)
    delta = bein("sihgc,sihgc->shgi", grad_att_seq, attended)
    grad_probs = bein("sihgc,sjhc->shgij", grad_att_seq, values)
    grad_scores = (probs_again * (grad_probs - delta[..., None])).astype(jnp.bfloat16)
    grad_qrot = (bein("shgij,sjhc->sihgc", grad_scores, key_rot) * inv_scale).reshape(
        seq_count, L, query_heads, HD
    )
    grad_krot = bein("shgij,sihgc->sjhc", grad_scores, query_rot) * inv_scale
    grad_value_act = bein("shgij,sihgc->sjhc", probs_bf, grad_att_seq)
    grad_qn = (grad_qrot * cosine + rotate_back(grad_qrot * sine)).reshape(
        row_count, query_heads, HD
    )
    grad_kn = (grad_krot * cosine + rotate_back(grad_krot * sine)).reshape(row_count, key_heads, HD)
    q_gain_part = jnp.sum(grad_qn * query_act * query_factor, axis=(0, 1))
    k_gain_part = jnp.sum(grad_kn * key_act * key_factor, axis=(0, 1))
    grad_query = (
        head_norm_back(grad_qn, query_act, query_factor, q_gain)
        .astype(jnp.bfloat16)
        .reshape(row_count, query_heads * HD)
    )
    grad_key = (
        head_norm_back(grad_kn, key_act, key_factor, k_gain)
        .astype(jnp.bfloat16)
        .reshape(row_count, key_heads * HD)
    )
    grad_value = grad_value_act.astype(jnp.bfloat16).reshape(row_count, key_heads * HD)
    query_term = matmul(normed_one.T, grad_query)
    key_term = matmul(normed_one.T, grad_key)
    value_term = matmul(normed_one.T, grad_value)
    grad_one_part = (
        matmul(grad_query, query_full.T)
        + matmul(grad_key, key_full.T)
        + matmul(grad_value, value_full.T)
    )
    grad_one = lax.psum_scatter(
        grad_one_part.astype(jnp.bfloat16), "gy", scatter_dimension=1, tiled=True
    ).astype(jnp.float32)
    query_grad, key_grad, value_grad, output_grad = (
        lax.psum_scatter(
            query_term.astype(jnp.bfloat16), "gx", scatter_dimension=0, tiled=True
        ).astype(jnp.float32),
        lax.psum_scatter(
            key_term.astype(jnp.bfloat16), "gx", scatter_dimension=0, tiled=True
        ).astype(jnp.float32),
        lax.psum_scatter(
            value_term.astype(jnp.bfloat16), "gx", scatter_dimension=0, tiled=True
        ).astype(jnp.float32),
        lax.psum_scatter(
            output_term.astype(jnp.bfloat16), "gx", scatter_dimension=1, tiled=True
        ).astype(jnp.float32),
    )
    in_share = layer_in.astype(jnp.float32)
    gain_share = lax.dynamic_slice_in_dim(attn_gain, column, part_width, 0)
    row_stat = lax.psum(jnp.sum(gain_share * grad_one * in_share, axis=1, keepdims=True), "gy")
    input_grad = (
        grad_mid_share
        + scale_one * gain_share * grad_one
        - in_share * scale_one**3 * (row_stat / D)
    )
    attn_gain_own = jnp.sum(grad_one * in_share * scale_one, axis=0)
    attn_gain_grad, mlp_gain_grad, q_gain_grad, k_gain_grad = lax.psum(
        (
            embed_share(attn_gain_own, column, D),
            embed_share(mlp_gain_own, column, D),
            q_gain_part,
            k_gain_part,
        ),
        ("gx", "gy"),
    )
    return (
        layer_out,
        input_grad,
        attn_gain_grad,
        q_gain_grad,
        k_gain_grad,
        query_grad,
        key_grad,
        value_grad,
        output_grad,
        mlp_gain_grad,
        gate_grad,
        up_grad,
        down_grad,
    )


def solution(mesh):
    placed = (
        P("gx", "gy"),
        P(),
        P(),
        P(),
        P("gx", "gy"),
        P("gx", "gy"),
        P("gx", "gy"),
        P("gy", "gx"),
        P(),
        P("gx", "gy"),
        P("gx", "gy"),
        P("gy", "gx"),
        P("gx", "gy"),
    )
    return jax.shard_map(
        on_device,
        mesh=mesh,
        in_specs=placed,
        out_specs=(
            P("gx", "gy"),
            P("gx", "gy"),
            P(),
            P(),
            P(),
            P("gx", "gy"),
            P("gx", "gy"),
            P("gx", "gy"),
            P("gy", "gx"),
            P(),
            P("gx", "gy"),
            P("gx", "gy"),
            P("gy", "gx"),
        ),
        check_vma=False,
    )
```

profile of v0, /device:TPU:0, one launch (start us, length us, event | category | flops | bytes accessed | tf_op | source)
XLA Modules:
  0.0 1706.3 jit_solution(14412919391294357786)
XLA Ops:
  12.6 34.2 %all-gather.10.cloned.1.call-done = bf16[1024,2048]{1,0:T(8,128)(2,1)} async-done(((bf16[1024,512]{1,0:T(8,128)(2,1)}), bf16[1024,2048]{1,0:T(8,128)(2,1)}) %all-gather.10.cloned.1.call-update) | async-done | bytes 4194320 | tf_op jit(solution)/shard_map/all_gather | solution.py:87
  46.8 3.2 fusion
  51.2 3.0 fusion.2
  54.2 43.8 %all-gather.16.cloned.1.call-done = bf16[2048,512]{1,0:T(8,128)(2,1)} async-done(((bf16[256,512]{1,0:T(8,128)(2,1)}), bf16[2048,512]{1,0:T(8,128)(2,1)}) %all-gather.16.cloned.1.call-update) | async-done | bytes 2097168 | tf_op jit(solution)/shard_map/all_gather | solution.py:94
  98.0 5.3 multiply_reduce_fusion.5
  103.3 2.8 reshape.272
  106.1 2.9 reshape.252
  109.0 30.0 %all-gather.14.cloned.1.call-done = bf16[2048,256]{1,0:T(8,128)(2,1)} async-done(((bf16[256,256]{1,0:T(8,128)(2,1)}), bf16[2048,256]{1,0:T(8,128)(2,1)}) %all-gather.14.cloned.1.call-update) | async-done | bytes 1048592 | tf_op jit(solution)/shard_map/all_gather | solution.py:95
  139.0 3.8 multiply_reduce_fusion.7
  144.4 35.6 %all-gather.12.cloned.1.call-done = bf16[2048,256]{1,0:T(8,128)(2,1)} async-done(((bf16[256,256]{1,0:T(8,128)(2,1)}), bf16[2048,256]{1,0:T(8,128)(2,1)}) %all-gather.12.cloned.1.call-update) | async-done | bytes 1048592 | tf_op jit(solution)/shard_map/all_gather | solution.py:96
  180.0 3.7 convolution_convert_fusion.9
  198.3 2.6 reshape.255
  200.9 30.0 %all-gather.18.cloned.1.call-done = bf16[512,2048]{1,0:T(8,128)(2,1)} async-done(((bf16[512,256]{1,0:T(8,128)(2,1)}), bf16[512,2048]{1,0:T(8,128)(2,1)}) %all-gather.18.cloned.1.call-update) | async-done | bytes 2097168 | tf_op jit(solution)/shard_map/all_gather | solution.py:97
  230.9 7.5 fusion.48
  241.4 148.3 %all-reduce.4.cloned.1.call-done = f32[1024,2048]{1,0:T(8,128)} async-done(((f32[1024,2048]{1,0:T(8,128)}), f32[1024,2048]{1,0:T(8,128)}) %all-reduce.4.cloned.1.call-update) | async-done | bytes 8388624 | tf_op jit(solution)/shard_map/psum | solution.py:125
  389.7 5.7 multiply_reduce_fusion.2
  395.4 3.3 copy-done
  398.7 2.8 multiply_convert_fusion
  401.6 89.2 %all-gather.20.cloned.1.call-done = bf16[2048,1536]{1,0:T(8,128)(2,1)} async-done(((bf16[256,1536]{1,0:T(8,128)(2,1)}), bf16[2048,1536]{1,0:T(8,128)(2,1)}) %all-gather.20.cloned.1.call-update) | async-done | bytes 6291472 | tf_op jit(solution)/shard_map/all_gather | solution.py:130
  490.7 11.7 fusion.49
  502.4 87.4 %all-gather.22.cloned.1.call-done = bf16[2048,1536]{1,0:T(8,128)(2,1)} async-done(((bf16[256,1536]{1,0:T(8,128)(2,1)}), bf16[2048,1536]{1,0:T(8,128)(2,1)}) %all-gather.22.cloned.1.call-update) | async-done | bytes 6291472 | tf_op jit(solution)/shard_map/all_gather | solution.py:131
  589.8 11.8 fusion.50
  601.6 22.5 %all-gather.26.cloned.1.call-done = bf16[1024,2048]{1,0:T(8,128)(2,1)} async-done(((bf16[1024,512]{1,0:T(8,128)(2,1)}), bf16[1024,2048]{1,0:T(8,128)(2,1)}) %all-gather.26.cloned.1.call-update) | async-done | bytes 4194320 | tf_op jit(solution)/shard_map/all_gather | solution.py:88
  624.1 101.4 %all-gather.24.cloned.1.call-done = bf16[1536,2048]{1,0:T(8,128)(2,1)} async-done(((bf16[1536,256]{1,0:T(8,128)(2,1)}), bf16[1536,2048]{1,0:T(8,128)(2,1)}) %all-gather.24.cloned.1.call-update) | async-done | bytes 6291472 | tf_op jit(solution)/shard_map/all_gather | solution.py:132
  725.5 16.4 multiply_convert_fusion.1
  741.9 10.0 fusion.51
  751.9 10.7 convolution_add_fusion
  764.0 149.8 %all-reduce.6.cloned.1.call-done = f32[1024,2048]{1,0:T(8,128)} async-done(((f32[1024,2048]{1,0:T(8,128)}), f32[1024,2048]{1,0:T(8,128)}) %all-reduce.6.cloned.1.call-update) | async-done | bytes 8388624 | tf_op jit(solution)/shard_map/psum | solution.py:152
  913.8 7.2 multiply_reduce_fusion
  923.3 4.6 multiply_subtract_fusion
  927.9 3.2 copy-done.1
  931.1 4.9 fusion.24
  937.4 2.5 copy.157
  941.9 6.8 fusion.28
  950.9 4.1 copy.171
  957.0 4.6 convolution_convert_fusion.6
  961.9 6.5 fusion.4
  977.6 11.0 convolution_convert_fusion.3
  992.5 4.3 convolution_multiply_fusion
  996.8 3.0 copy.151
  999.8 4.7 copy.145
  1006.3 3.2 copy.148
  1009.5 3.2 copy.149
  1012.7 5.9 multiply_reduce_fusion.4
  1018.6 3.0 copy.150
  1026.1 3.8 convolution_convert_fusion.5
  1030.0 7.2 convolution_convert_fusion.4
  1041.6 3.3 add_convert_fusion
  1045.1 11.5 convolution_convert_fusion.2
  1056.8 11.5 convolution_convert_fusion.1
  1068.4 11.3 convolution_convert_fusion
  1082.4 11.0 reduce-scatter.16.cloned.1.call-done
  1095.0 44.2 %reduce-scatter.10.cloned.1.call-done = bf16[1024,512]{1,0:T(8,128)(2,1)} async-done(((bf16[1024,2048]{1,0:T(8,128)(2,1)}), bf16[1024,512]{1,0:T(8,128)(2,1)}) %reduce-scatter.10.cloned.1.call-update) | async-done | bytes 1048592 | tf_op jit(solution)/shard_map/reduce_scatter | solution.py:138
  1139.2 3.2 add_convert_fusion.1
  1142.4 69.1 %reduce-scatter.14.cloned.1.call-done = bf16[256,512]{1,0:T(8,128)(2,1)} async-done(((bf16[2048,512]{1,0:T(8,128)(2,1)}), bf16[256,512]{1,0:T(8,128)(2,1)}) %reduce-scatter.14.cloned.1.call-update) | async-done | bytes 262160 | tf_op jit(solution)/shard_map/reduce_scatter | solution.py:217
  1213.3 69.6 %reduce-scatter.20.cloned.1.call-done = bf16[512,256]{1,0:T(8,128)(2,1)} async-done(((bf16[512,2048]{1,0:T(8,128)(2,1)}), bf16[512,256]{1,0:T(8,128)(2,1)}) %reduce-scatter.20.cloned.1.call-update) | async-done | bytes 262160 | tf_op jit(solution)/shard_map/reduce_scatter | solution.py:226
  1284.7 43.9 %reduce-scatter.12.cloned.1.call-done = bf16[1024,512]{1,0:T(8,128)(2,1)} async-done(((bf16[1024,2048]{1,0:T(8,128)(2,1)}), bf16[1024,512]{1,0:T(8,128)(2,1)}) %reduce-scatter.12.cloned.1.call-update) | async-done | bytes 1048592 | tf_op jit(solution)/shard_map/reduce_scatter | solution.py:213
  1331.2 118.9 %reduce-scatter.22.cloned.1.call-done = bf16[256,1536]{1,0:T(8,128)(2,1)} async-done(((bf16[2048,1536]{1,0:T(8,128)(2,1)}), bf16[256,1536]{1,0:T(8,128)(2,1)}) %reduce-scatter.22.cloned.1.call-update) | async-done | bytes 786448 | tf_op jit(solution)/shard_map/reduce_scatter | solution.py:165
  1452.6 118.4 %reduce-scatter.24.cloned.1.call-done = bf16[256,1536]{1,0:T(8,128)(2,1)} async-done(((bf16[2048,1536]{1,0:T(8,128)(2,1)}), bf16[256,1536]{1,0:T(8,128)(2,1)}) %reduce-scatter.24.cloned.1.call-update) | async-done | bytes 786448 | tf_op jit(solution)/shard_map/reduce_scatter | solution.py:168
  1571.1 2.5 convert_element_type.161
  1573.5 43.1 %all-reduce = (f32[2048]{0:T(1024)}, f32[128]{0:T(128)}, f32[128]{0:T(128)}, f32[2048]{0:T(1024)}) all-reduce(f32[2048]{0:T(1024)S(1)} %dynamic_update_slice.6, f32[128]{0:T(128)S(1)} %bitcast_reduce_fusion, f32[128]{0:T(128)S(1)} %get-tuple-element.21, ...), channel_id=1, replica_groups=mesh['gx'=8,'gy'=4] {'gx','gy'}, use_global_device_ids=true, to_apply=%region_16.17 | all-reduce | flops 4352 | bytes 34816 | tf_op jit(solution)/shard_map/psum | solution.py:239
  1616.6 6.6 psum.51
  1623.1 70.1 %reduce-scatter.26.cloned.1.call-done = bf16[1536,256]{1,0:T(8,128)(2,1)} async-done(((bf16[1536,2048]{1,0:T(8,128)(2,1)}), bf16[1536,256]{1,0:T(8,128)(2,1)}) %reduce-scatter.26.cloned.1.call-update) | async-done | bytes 786448 | tf_op jit(solution)/shard_map/reduce_scatter | solution.py:171
  1695.7 3.5 fusion.8
  (217 shorter events, 76.0 us)
Async XLA Ops:
  7.2 44.0 %copy-start.48 = (f32[2048]{0:T(1024)S(1)}, f32[2048]{0:T(1024)}, u32[]{:S(2)}) copy-start(f32[2048]{0:T(1024)} %param.14) | copy-start | bytes 24580
  7.2 39.6 %all-gather.10.cloned.1.call-start = ((), (), s32[]{:S(2)}) async-start(), calls=%async_computation.9 | async-start | bytes 5242880 | tf_op jit(solution)/shard_map/all_gather | solution.py:87
  7.9 90.1 %all-gather.16.cloned.1.call-start = ((), (), s32[]{:S(2)}) async-start(), calls=%async_computation.12 | async-start | bytes 2359296 | tf_op jit(solution)/shard_map/all_gather | solution.py:94
  8.7 130.3 %all-gather.14.cloned.1.call-start = ((), (), s32[]{:S(2)}) async-start(), calls=%async_computation.11 | async-start | bytes 1179648 | tf_op jit(solution)/shard_map/all_gather | solution.py:95
  9.4 170.6 %all-gather.12.cloned.1.call-start = ((), (), s32[]{:S(2)}) async-start(), calls=%async_computation.10 | async-start | bytes 1179648 | tf_op jit(solution)/shard_map/all_gather | solution.py:96
  10.0 221.0 %all-gather.18.cloned.1.call-start = ((), (), s32[]{:S(2)}) async-start(), calls=%async_computation.13 | async-start | bytes 2359296 | tf_op jit(solution)/shard_map/all_gather | solution.py:97
  10.6 379.1 %all-reduce.4.cloned.1.call-start = ((), (), s32[]{:S(2)}) async-start(), calls=%async_computation.14 | async-start | bytes 16777216 | tf_op jit(solution)/shard_map/psum | solution.py:125
  46.8 4.4 copy-start.2
  103.3 5.7 copy-start.4
  144.3 41.8 %copy-start.41 = (f32[1024,4]{0,1:T(4,128)}, f32[1024,4]{0,1:T(4,128)S(1)}, u32[]{:S(2)}) copy-start(f32[1024,4]{0,1:T(4,128)S(1)} %get-tuple-element.45) | copy-start | bytes 49156
  144.4 40.3 %copy-start.51 = (f32[128]{0:T(128)S(1)}, f32[128]{0:T(128)}, u32[]{:S(2)}) copy-start(f32[128]{0:T(128)} %param.16) | copy-start | bytes 1540
  183.7 2.4 copy-start.49
  186.1 2.7 copy-start.16
  190.5 3.3 copy-start.6
  190.5 3.3 copy-start.40
  196.2 42.3 %copy-start.19 = (bf16[2,2,128,2,512]{4,2,3,1,0:T(8,128)(2,1)}, bf16[2,2,128,2,512]{4,2,3,1,0:T(8,128)(2,1)S(1)}, u32[]{:S(2)}) copy-start(bf16[2,2,128,2,512]{4,2,3,1,0:T(8,128)(2,1)S(1)} %convolution_convert_fusion.8) | copy-start | bytes 3145732
  238.5 252.3 %all-gather.20.cloned.1.call-start = ((), (), s32[]{:S(2)}) async-start(), calls=%async_computation.15 | async-start | bytes 7077888 | tf_op jit(solution)/shard_map/all_gather | solution.py:130
  239.2 350.6 %all-gather.22.cloned.1.call-start = ((), (), s32[]{:S(2)}) async-start(), calls=%async_computation.16 | async-start | bytes 7077888 | tf_op jit(solution)/shard_map/all_gather | solution.py:131
  240.0 384.1 %all-gather.26.cloned.1.call-start = ((), (), s32[]{:S(2)}) async-start(), calls=%async_computation.19 | async-start | bytes 5242880 | tf_op jit(solution)/shard_map/all_gather | solution.py:88
  240.7 484.8 %all-gather.24.cloned.1.call-start = ((), (), s32[]{:S(2)}) async-start(), calls=%async_computation.17 | async-start | bytes 7077888 | tf_op jit(solution)/shard_map/all_gather | solution.py:132
  241.3 157.4 %copy-start.43 = (f32[2048]{0:T(1024)S(1)}, f32[2048]{0:T(1024)}, u32[]{:S(2)}) copy-start(f32[2048]{0:T(1024)} %param.21) | copy-start | bytes 24580
  241.3 672.5 %all-reduce.6.cloned.1.call-start = ((), (), s32[]{:S(2)}) async-start(), calls=%async_computation.20 | async-start | bytes 16777216 | tf_op jit(solution)/shard_map/psum | solution.py:152
  395.4 3.3 copy-start
  741.9 10.0 copy-start.54
  741.9 10.0 copy-start.52
  762.6 318.1 %reduce-scatter.18.cloned.1.call-start = ((), (), s32[]{:S(2)}) async-start(), calls=%async_computation.24 | async-start | bytes 1179648 | tf_op jit(solution)/shard_map/reduce_scatter | solution.py:223
  913.8 8.2 copy-start.3
  913.8 9.4 copy-start.18
  927.9 3.2 copy-start.1
  948.8 6.2 copy-start.20
  961.6 6.8 copy-start.11
  961.6 131.8 %reduce-scatter.16.cloned.1.call-start = ((), (), s32[]{:S(2)}) async-start(), calls=%async_computation.23 | async-start | bytes 1179648 | tf_op jit(solution)/shard_map/reduce_scatter | solution.py:220
  961.9 6.6 copy-start.15
  968.4 2.1 copy-start.8
  968.4 2.2 copy-start.39
  971.1 2.3 copy-start.21
  972.4 2.7 copy-start.23
  975.1 2.4 copy-start.55
  977.5 161.7 %reduce-scatter.10.cloned.1.call-start = ((), (), s32[]{:S(2)}) async-start(), calls=%async_computation.18 | async-start | bytes 5242880 | tf_op jit(solution)/shard_map/reduce_scatter | solution.py:138
  988.6 2.1 copy-start.50
  988.6 2.1 copy-start.5
  988.6 3.9 copy-start.17
  988.6 222.9 %reduce-scatter.14.cloned.1.call-start = ((), (), s32[]{:S(2)}) async-start(), calls=%async_computation.22 | async-start | bytes 2359296 | tf_op jit(solution)/shard_map/reduce_scatter | solution.py:217
  996.8 7.7 copy-start.27
  999.8 4.7 copy-start.7
  1018.5 5.3 copy-start.34
  1018.6 5.3 copy-start.42
  1018.6 5.3 copy-start.44
  1021.6 2.3 copy-start.13
  1023.8 2.3 copy-start.24
  1026.1 3.9 copy-start.30
  1029.9 7.6 copy-start.32
  1029.9 7.6 copy-start.35
  1029.9 253.0 %reduce-scatter.20.cloned.1.call-start = ((), (), s32[]{:S(2)}) async-start(), calls=%async_computation.25 | async-start | bytes 2359296 | tf_op jit(solution)/shard_map/reduce_scatter | solution.py:226
  1037.3 291.4 %reduce-scatter.12.cloned.1.call-start = ((), (), s32[]{:S(2)}) async-start(), calls=%async_computation.21 | async-start | bytes 5242880 | tf_op jit(solution)/shard_map/reduce_scatter | solution.py:213
  1039.2 2.4 copy-start.33
  1039.2 2.4 copy-start.36
  1045.0 405.1 %reduce-scatter.22.cloned.1.call-start = ((), (), s32[]{:S(2)}) async-start(), calls=%async_computation.26 | async-start | bytes 7077888 | tf_op jit(solution)/shard_map/reduce_scatter | solution.py:165
  1056.6 514.5 %reduce-scatter.24.cloned.1.call-start = ((), (), s32[]{:S(2)}) async-start(), calls=%async_computation.27 | async-start | bytes 7077888 | tf_op jit(solution)/shard_map/reduce_scatter | solution.py:168
  1068.3 625.0 %reduce-scatter.26.cloned.1.call-start = ((), (), s32[]{:S(2)}) async-start(), calls=%async_computation.28 | async-start | bytes 7077888 | tf_op jit(solution)/shard_map/reduce_scatter | solution.py:171
  1079.7 249.0 %copy-start.9 = (bf16[1024,512]{1,0:T(8,128)(2,1)S(1)}, bf16[1024,512]{1,0:T(8,128)(2,1)}, u32[]{:S(2)}) copy-start(bf16[1024,512]{1,0:T(8,128)(2,1)} %param.13) | copy-start | bytes 3145732
  1079.7 249.0 %copy-start.46 = (f32[1024]{0:T(1024)S(1)}, f32[1024]{0:T(1024)}, u32[]{:S(2)}) copy-start(f32[1024]{0:T(1024)} %copy-done.45) | copy-start | bytes 12292
  1284.7 411.0 %copy-start.47 = (f32[1024]{0:T(1024)S(1)}, f32[1024]{0:T(1024)}, u32[]{:S(2)}) copy-start(f32[1024]{0:T(1024)} %get-tuple-element.48) | copy-start | bytes 12292
  1328.7 367.0 %copy-start.25 = (bf16[1024,512]{1,0:T(8,128)(2,1)S(1)}, bf16[1024,512]{1,0:T(8,128)(2,1)}, u32[]{:S(2)}) copy-start(bf16[1024,512]{1,0:T(8,128)(2,1)} %reduce-scatter.12.cloned.1.call-done) | copy-start | bytes 3145732
  (12 other events, 14.9 us)
Sparse Core Ops, SparseCore 0:
  9.6 37.1 all-gather.9
  48.9 49.0 all-gather.15
  100.1 38.7 all-gather.13
  141.0 38.9 all-gather.11
  181.9 49.0 all-gather.17
  238.6 151.0 all-reduce.3
  391.9 98.8 all-gather.19
  492.9 96.8 all-gather.21
  591.4 32.6 all-gather.25
  626.0 99.4 all-gather.23
  762.8 151.0 all-reduce.5
  961.7 64.4 reduce-scatter.17
  1030.2 63.1 reduce-scatter.15
  1095.7 43.3 reduce-scatter.9
  1143.1 68.3 reduce-scatter.13
  1214.9 67.9 reduce-scatter.19
  1285.3 43.2 reduce-scatter.11
  1332.1 118.0 reduce-scatter.21
  1453.7 117.2 reduce-scatter.23
  1574.5 118.7 reduce-scatter.25
where the time goes:
time: 1710 us
  waiting for transfers between devices  1320 us (77%)
  matrix products  179 us (10%)
  other arithmetic  71 us (4%)
  local copies, waits for them, and re-layouts  65.8 us (4%)
  blocking collectives  49.6 us (3%)
    dot_general x21, matrix products, matmul(): return jnp.dot(left, right, preferred_element_type=jnp.float32)  156 us
    psum x1, waiting for transfers between devices, on_device(): grad_two = lax.psum(grad_two_part, 'gy')  150 us
    psum x1, waiting for transfers between devices, on_device(): attn_sum = lax.psum(matmul(attended_flat, output_full), 'gy')  148 us
    reduce_scatter x1, waiting for transfers between devices, on_device(): lax.psum_scatter(gate_term.astype(jnp.bfloat16), 'gx', scatter_dimension=...  119 us
    reduce_scatter x1, waiting for transfers between devices, on_device(): lax.psum_scatter(up_term.astype(jnp.bfloat16), 'gx', scatter_dimension=0,...  118 us
    all_gather x1, waiting for transfers between devices, on_device(): lax.all_gather(w_down, 'gx', axis=1, tiled=True)  101 us
    all_gather x1, waiting for transfers between devices, on_device(): lax.all_gather(w_gate, 'gx', axis=0, tiled=True)  89.2 us
    all_gather x1, waiting for transfers between devices, on_device(): lax.all_gather(w_up, 'gx', axis=0, tiled=True)  87.4 us
  transfers between devices with their start and end apart: 20, of which 19 were waited for; matrix products, arithmetic and copies ran while one was open for 12% of the time, Pallas kernels for 0%

commit v1 on v0

--- a/solution.py
+++ b/solution.py
@@ -11,6 +11,18 @@
 L = 512
 epsilon = 1e-06
 rope_base = 1000000.0
+
+
+def collect(x, axis, dim):
+    ways, here = (lax.axis_size(axis), lax.axis_index(axis))
+    grown, reach = (x, 1)
+    while reach < ways:
+        theirs = lax.ppermute(grown, axis, [(d, d ^ reach) for d in range(ways)])
+        mine_first = jnp.concatenate([grown, theirs], axis=dim)
+        theirs_first = jnp.concatenate([theirs, grown], axis=dim)
+        grown = jnp.where(here & reach == 0, mine_first, theirs_first)
+        reach = 2 * reach
+    return grown
 
 
 def rope_tables(length, dim_width):
@@ -129,7 +141,7 @@
     gate_full, up_full, down_full = (
         lax.all_gather(w_gate, "gx", axis=0, tiled=True),
         lax.all_gather(w_up, "gx", axis=0, tiled=True),
-        lax.all_gather(w_down, "gx", axis=1, tiled=True),
+        collect(w_down, "gx", 1),
     )
     gate_act = matmul(normed_two, gate_full)
     up_act = matmul(normed_two, up_full)

time: 1710 us -> 1640 us (0.959)
  waiting for transfers between devices: 1320 us -> 1240 us
    all_gather x1 -> x0, waiting for transfers between devices: 101 us -> none  [on_device(): lax.all_gather(w_down, 'gx', axis=1, tiled=True)]
    psum x1, waiting for transfers between devices: 148 us -> 86.2 us  [on_device(): attn_sum = lax.psum(matmul(attended_flat, output_full), 'gy')]
    ppermute x0 -> x3, waiting for transfers between devices: none -> 53 us  [collect(): theirs = lax.ppermute(grown, axis, [(d, d ^ reach) for d in range(ways)])]
    all_gather x1, waiting for transfers between devices: 89.2 us -> 115 us  [on_device(): lax.all_gather(w_gate, 'gx', axis=0, tiled=True)]
  transfers between devices with their start and end apart: 20 -> 22, of which waited for: 19 -> 20; matrix products, arithmetic and copies ran while one was open for 12% -> 13% of each run, Pallas kernels for 0% -> 0%
where the time goes in v1:
time: 1640 us; the launch traced here: 1630 us
  waiting for transfers between devices  1240 us (76%)
  matrix products  181 us (11%)
  other arithmetic  79.6 us (5%)
  local copies, waits for them, and re-layouts  65.8 us (4%)
  blocking collectives  49.6 us (3%)
    dot_general x21, matrix products, matmul(): return jnp.dot(left, right, preferred_element_type=jnp.float32)  158 us
    psum x1, waiting for transfers between devices, on_device(): grad_two = lax.psum(grad_two_part, 'gy')  152 us
    reduce_scatter x1, waiting for transfers between devices, on_device(): lax.psum_scatter(gate_term.astype(jnp.bfloat16), 'gx', scatter_dimension=...  119 us
    reduce_scatter x1, waiting for transfers between devices, on_device(): lax.psum_scatter(up_term.astype(jnp.bfloat16), 'gx', scatter_dimension=0,...  118 us
    all_gather x1, waiting for transfers between devices, on_device(): lax.all_gather(w_gate, 'gx', axis=0, tiled=True)  115 us
    all_gather x1, waiting for transfers between devices, on_device(): lax.all_gather(w_up, 'gx', axis=0, tiled=True)  88.2 us
    psum x1, waiting for transfers between devices, on_device(): attn_sum = lax.psum(matmul(attended_flat, output_full), 'gy')  86.2 us
    reduce_scatter x1, waiting for transfers between devices, on_device(): lax.psum_scatter(down_term.astype(jnp.bfloat16), 'gx', scatter_dimension=...  70.3 us
  transfers between devices with their start and end apart: 22, of which 20 were waited for; matrix products, arithmetic and copies ran while one was open for 13% of the time, Pallas kernels for 0%

profile of v1, /device:TPU:0, one launch (start us, length us, event | category | flops | bytes accessed | tf_op | source)
XLA Modules:
  0.0 1632.7 jit_solution(4807874665334473795)
XLA Ops:
  12.5 34.3 %all-gather.9.cloned.1.call-done = bf16[1024,2048]{1,0:T(8,128)(2,1)} async-done(((bf16[1024,512]{1,0:T(8,128)(2,1)}), bf16[1024,2048]{1,0:T(8,128)(2,1)}) %all-gather.9.cloned.1.call-update) | async-done | bytes 4194320 | tf_op jit(solution)/shard_map/all_gather | solution.py:99
  46.8 3.2 fusion
  51.2 3.0 fusion.2
  54.2 43.8 %all-gather.15.cloned.1.call-done = bf16[2048,512]{1,0:T(8,128)(2,1)} async-done(((bf16[256,512]{1,0:T(8,128)(2,1)}), bf16[2048,512]{1,0:T(8,128)(2,1)}) %all-gather.15.cloned.1.call-update) | async-done | bytes 2097168 | tf_op jit(solution)/shard_map/all_gather | solution.py:106
  98.0 5.3 multiply_reduce_fusion.5
  103.3 2.8 reshape.272
  106.1 2.9 reshape.252
  109.0 30.0 %all-gather.13.cloned.1.call-done = bf16[2048,256]{1,0:T(8,128)(2,1)} async-done(((bf16[256,256]{1,0:T(8,128)(2,1)}), bf16[2048,256]{1,0:T(8,128)(2,1)}) %all-gather.13.cloned.1.call-update) | async-done | bytes 1048592 | tf_op jit(solution)/shard_map/all_gather | solution.py:107
  139.0 3.8 multiply_reduce_fusion.7
  145.0 35.0 %all-gather.11.cloned.1.call-done = bf16[2048,256]{1,0:T(8,128)(2,1)} async-done(((bf16[256,256]{1,0:T(8,128)(2,1)}), bf16[2048,256]{1,0:T(8,128)(2,1)}) %all-gather.11.cloned.1.call-update) | async-done | bytes 1048592 | tf_op jit(solution)/shard_map/all_gather | solution.py:108
  180.0 3.7 convolution_convert_fusion.9
  200.8 30.2 %all-gather.17.cloned.1.call-done = bf16[512,2048]{1,0:T(8,128)(2,1)} async-done(((bf16[512,256]{1,0:T(8,128)(2,1)}), bf16[512,2048]{1,0:T(8,128)(2,1)}) %all-gather.17.cloned.1.call-update) | async-done | bytes 2097168 | tf_op jit(solution)/shard_map/all_gather | solution.py:109
  231.0 7.5 fusion.56
  241.7 17.8 %collective-permute-done = bf16[1536,256]{1,0:T(8,128)(2,1)} collective-permute-done((bf16[1536,256]{1,0:T(8,128)(2,1)S(1)}, bf16[1536,256]{1,0:T(8,128)(2,1)}, u32[]{:S(2)}, u32[]{:S(2)}) %collective-permute-start) | collective-permute-done | bytes 786464 | tf_op jit(solution)/shard_map/ppermute | solution.py:20
  259.4 2.9 maximum_select_fusion.2
  262.4 35.3 %collective-permute-done.1 = bf16[1536,512]{1,0:T(8,128)(2,1)} collective-permute-done((bf16[1536,512]{1,0:T(8,128)(2,1)}, bf16[1536,512]{1,0:T(8,128)(2,1)}, u32[]{:S(2)}, u32[]{:S(2)}) %collective-permute-start.1) | collective-permute-done | bytes 1572896 | tf_op jit(solution)/shard_map/ppermute | solution.py:20
  297.7 5.1 maximum_select_fusion.1
  303.6 86.2 %all-reduce.4.cloned.1.call-done = f32[1024,2048]{1,0:T(8,128)} async-done(((f32[1024,2048]{1,0:T(8,128)}), f32[1024,2048]{1,0:T(8,128)}) %all-reduce.4.cloned.1.call-update) | async-done | bytes 8388624 | tf_op jit(solution)/shard_map/psum | solution.py:137
  389.8 5.7 multiply_reduce_fusion.2
  395.6 3.3 copy-done
  398.8 2.7 multiply_convert_fusion
  401.6 114.7 %all-gather.19.cloned.1.call-done = bf16[2048,1536]{1,0:T(8,128)(2,1)} async-done(((bf16[256,1536]{1,0:T(8,128)(2,1)}), bf16[2048,1536]{1,0:T(8,128)(2,1)}) %all-gather.19.cloned.1.call-update) | async-done | bytes 6291472 | tf_op jit(solution)/shard_map/all_gather | solution.py:142
  516.3 11.8 fusion.57
  528.0 88.2 %all-gather.21.cloned.1.call-done = bf16[2048,1536]{1,0:T(8,128)(2,1)} async-done(((bf16[256,1536]{1,0:T(8,128)(2,1)}), bf16[2048,1536]{1,0:T(8,128)(2,1)}) %all-gather.21.cloned.1.call-update) | async-done | bytes 6291472 | tf_op jit(solution)/shard_map/all_gather | solution.py:143
  616.2 11.7 fusion.58
  628.0 22.5 %all-gather.23.cloned.1.call-done = bf16[1024,2048]{1,0:T(8,128)(2,1)} async-done(((bf16[1024,512]{1,0:T(8,128)(2,1)}), bf16[1024,2048]{1,0:T(8,128)(2,1)}) %all-gather.23.cloned.1.call-update) | async-done | bytes 4194320 | tf_op jit(solution)/shard_map/all_gather | solution.py:100
  650.5 17.7 %fusion.10 = (bf16[1024,1536]{1,0:T(8,128)(2,1)}, bf16[1024,1536]{1,0:T(8,128)(2,1)}, bf16[1024,1536]{1,0:T(8,128)(2,1)}) fusion(f32[1024,1536]{1,0:T(8,128)} %fusion.57, f32[1024,1536]{1,0:T(8,128)} %fusion.58, bf16[1024,2048]{1,0:T(8,128)(2,1)} %all-gather.23.cloned.1.call-done, bf16[1536,1024]{1,0:T(8,128)(2,1)} %collective-permute-done.2, ...), kind=kOutput, calls=%fused_computation.29 | convolution fusion | flops 6495928320 | bytes 32505856 | tf_op jit(solution)/shard_map/dot_general | solution.py:59
  668.2 9.9 fusion.59
  678.1 8.8 convolution_add_fusion
  688.4 151.7 %all-reduce.6.cloned.1.call-done = f32[1024,2048]{1,0:T(8,128)} async-done(((f32[1024,2048]{1,0:T(8,128)}), f32[1024,2048]{1,0:T(8,128)}) %all-reduce.6.cloned.1.call-update) | async-done | bytes 8388624 | tf_op jit(solution)/shard_map/psum | solution.py:164
  840.0 7.4 multiply_reduce_fusion
  849.5 4.6 multiply_subtract_fusion
  854.1 3.3 copy-done.1
  857.4 4.9 fusion.29
  868.2 6.8 fusion.33
  877.1 4.1 copy.177
  883.2 4.7 convolution_convert_fusion.6
  887.9 5.8 fusion.4
  903.0 13.4 convolution_convert_fusion.3
  920.4 4.2 convolution_multiply_fusion
  924.6 3.0 copy.156
  927.6 4.7 copy.150
  934.2 3.2 copy.153
  937.3 3.2 copy.154
  940.5 5.8 multiply_reduce_fusion.4
  946.4 3.0 copy.155
  953.8 3.8 convolution_convert_fusion.5
  957.7 7.2 convolution_convert_fusion.4
  969.4 3.3 add_convert_fusion
  972.8 11.6 convolution_convert_fusion.2
  984.7 11.5 convolution_convert_fusion.1
  996.3 11.3 convolution_convert_fusion
  1010.4 9.0 reduce-scatter.16.cloned.1.call-done
  1021.0 44.3 %reduce-scatter.10.cloned.1.call-done = bf16[1024,512]{1,0:T(8,128)(2,1)} async-done(((bf16[1024,2048]{1,0:T(8,128)(2,1)}), bf16[1024,512]{1,0:T(8,128)(2,1)}) %reduce-scatter.10.cloned.1.call-update) | async-done | bytes 1048592 | tf_op jit(solution)/shard_map/reduce_scatter | solution.py:150
  1065.2 3.2 add_convert_fusion.1
  1068.5 69.5 %reduce-scatter.14.cloned.1.call-done = bf16[256,512]{1,0:T(8,128)(2,1)} async-done(((bf16[2048,512]{1,0:T(8,128)(2,1)}), bf16[256,512]{1,0:T(8,128)(2,1)}) %reduce-scatter.14.cloned.1.call-update) | async-done | bytes 262160 | tf_op jit(solution)/shard_map/reduce_scatter | solution.py:229
  1139.8 69.6 %reduce-scatter.20.cloned.1.call-done = bf16[512,256]{1,0:T(8,128)(2,1)} async-done(((bf16[512,2048]{1,0:T(8,128)(2,1)}), bf16[512,256]{1,0:T(8,128)(2,1)}) %reduce-scatter.20.cloned.1.call-update) | async-done | bytes 262160 | tf_op jit(solution)/shard_map/reduce_scatter | solution.py:238
  1211.2 44.0 %reduce-scatter.12.cloned.1.call-done = bf16[1024,512]{1,0:T(8,128)(2,1)} async-done(((bf16[1024,2048]{1,0:T(8,128)(2,1)}), bf16[1024,512]{1,0:T(8,128)(2,1)}) %reduce-scatter.12.cloned.1.call-update) | async-done | bytes 1048592 | tf_op jit(solution)/shard_map/reduce_scatter | solution.py:225
  1257.7 118.9 %reduce-scatter.22.cloned.1.call-done = bf16[256,1536]{1,0:T(8,128)(2,1)} async-done(((bf16[2048,1536]{1,0:T(8,128)(2,1)}), bf16[256,1536]{1,0:T(8,128)(2,1)}) %reduce-scatter.22.cloned.1.call-update) | async-done | bytes 786448 | tf_op jit(solution)/shard_map/reduce_scatter | solution.py:177
  1379.1 118.3 %reduce-scatter.24.cloned.1.call-done = bf16[256,1536]{1,0:T(8,128)(2,1)} async-done(((bf16[2048,1536]{1,0:T(8,128)(2,1)}), bf16[256,1536]{1,0:T(8,128)(2,1)}) %reduce-scatter.24.cloned.1.call-update) | async-done | bytes 786448 | tf_op jit(solution)/shard_map/reduce_scatter | solution.py:180
  1499.9 43.2 %all-reduce = (f32[2048]{0:T(1024)}, f32[128]{0:T(128)}, f32[128]{0:T(128)}, f32[2048]{0:T(1024)}) all-reduce(f32[2048]{0:T(1024)S(1)} %dynamic_update_slice.6, f32[128]{0:T(128)S(1)} %bitcast_reduce_fusion, f32[128]{0:T(128)S(1)} %get-tuple-element.21, ...), channel_id=1, replica_groups=mesh['gx'=8,'gy'=4] {'gx','gy'}, use_global_device_ids=true, to_apply=%region_16.17 | all-reduce | flops 4352 | bytes 34816 | tf_op jit(solution)/shard_map/psum | solution.py:251
  1543.0 6.5 psum.51
  1549.5 70.3 %reduce-scatter.26.cloned.1.call-done = bf16[1536,256]{1,0:T(8,128)(2,1)} async-done(((bf16[1536,2048]{1,0:T(8,128)(2,1)}), bf16[1536,256]{1,0:T(8,128)(2,1)}) %reduce-scatter.26.cloned.1.call-update) | async-done | bytes 786448 | tf_op jit(solution)/shard_map/reduce_scatter | solution.py:183
  1622.2 3.5 fusion.13
  (236 shorter events, 84.8 us)
Async XLA Ops:
  7.2 44.0 %copy-start.55 = (f32[2048]{0:T(1024)S(1)}, f32[2048]{0:T(1024)}, u32[]{:S(2)}) copy-start(f32[2048]{0:T(1024)} %param.14) | copy-start | bytes 24580
  7.2 39.6 %all-gather.9.cloned.1.call-start = ((), (), s32[]{:S(2)}) async-start(), calls=%async_computation.9 | async-start | bytes 5242880 | tf_op jit(solution)/shard_map/all_gather | solution.py:99
  7.9 90.1 %all-gather.15.cloned.1.call-start = ((), (), s32[]{:S(2)}) async-start(), calls=%async_computation.12 | async-start | bytes 2359296 | tf_op jit(solution)/shard_map/all_gather | solution.py:106
  8.7 130.3 %all-gather.13.cloned.1.call-start = ((), (), s32[]{:S(2)}) async-start(), calls=%async_computation.11 | async-start | bytes 1179648 | tf_op jit(solution)/shard_map/all_gather | solution.py:107
  9.4 170.6 %all-gather.11.cloned.1.call-start = ((), (), s32[]{:S(2)}) async-start(), calls=%async_computation.10 | async-start | bytes 1179648 | tf_op jit(solution)/shard_map/all_gather | solution.py:108
  10.0 221.0 %all-gather.17.cloned.1.call-start = ((), (), s32[]{:S(2)}) async-start(), calls=%async_computation.13 | async-start | bytes 2359296 | tf_op jit(solution)/shard_map/all_gather | solution.py:109
  10.6 379.2 %all-reduce.4.cloned.1.call-start = ((), (), s32[]{:S(2)}) async-start(), calls=%async_computation.14 | async-start | bytes 16777216 | tf_op jit(solution)/shard_map/psum | solution.py:137
  12.5 172.5 %copy-start.26 = (f32[512,128]{0,1:T(8,128)}, f32[512,128]{0,1:T(8,128)S(1)}, u32[]{:S(2)}) copy-start(f32[512,128]{0,1:T(8,128)S(1)} %get-tuple-element.42) | copy-start | bytes 786436
  12.5 172.5 %copy-start.29 = (f32[512,128]{0,1:T(8,128)}, f32[512,128]{0,1:T(8,128)S(1)}, u32[]{:S(2)}) copy-start(f32[512,128]{0,1:T(8,128)S(1)} %get-tuple-element.43) | copy-start | bytes 786436
  46.8 4.4 copy-start.2
  103.3 5.7 copy-start.4
  143.7 41.3 %copy-start.8 = (f32[2,512,2,128]{1,0,3,2:T(2,128)}, f32[2,512,2,128]{1,0,3,2:T(2,128)S(1)}, u32[]{:S(2)}) copy-start(f32[2,512,2,128]{1,0,3,2:T(2,128)S(1)} %reshape.250) | copy-start | bytes 3145732
  144.4 40.6 %copy-start.47 = (f32[1024,2]{0,1:T(2,128)}, f32[1024,2]{0,1:T(2,128)S(1)}, u32[]{:S(2)}) copy-start(f32[1024,2]{0,1:T(2,128)S(1)} %get-tuple-element.47) | copy-start | bytes 24580
  145.0 40.5 %copy-start.45 = (f32[1024,4]{0,1:T(4,128)}, f32[1024,4]{0,1:T(4,128)S(1)}, u32[]{:S(2)}) copy-start(f32[1024,4]{0,1:T(4,128)S(1)} %get-tuple-element.45) | copy-start | bytes 49156
  145.0 39.6 %copy-start.58 = (f32[128]{0:T(128)S(1)}, f32[128]{0:T(128)}, u32[]{:S(2)}) copy-start(f32[128]{0:T(128)} %param.16) | copy-start | bytes 1540
  185.4 3.3 copy-start.16
  190.3 3.3 copy-start.6
  190.3 3.3 copy-start.43
  196.1 42.5 %copy-start.19 = (bf16[2,2,128,2,512]{4,2,3,1,0:T(8,128)(2,1)}, bf16[2,2,128,2,512]{4,2,3,1,0:T(8,128)(2,1)S(1)}, u32[]{:S(2)}) copy-start(bf16[2,2,128,2,512]{4,2,3,1,0:T(8,128)(2,1)S(1)} %convolution_convert_fusion.8) | copy-start | bytes 3145732
  238.6 277.7 %all-gather.19.cloned.1.call-start = ((), (), s32[]{:S(2)}) async-start(), calls=%async_computation.15 | async-start | bytes 7077888 | tf_op jit(solution)/shard_map/all_gather | solution.py:142
  239.3 376.9 %all-gather.21.cloned.1.call-start = ((), (), s32[]{:S(2)}) async-start(), calls=%async_computation.16 | async-start | bytes 7077888 | tf_op jit(solution)/shard_map/all_gather | solution.py:143
  240.1 410.4 %all-gather.23.cloned.1.call-start = ((), (), s32[]{:S(2)}) async-start(), calls=%async_computation.18 | async-start | bytes 5242880 | tf_op jit(solution)/shard_map/all_gather | solution.py:100
  240.2 19.3 %collective-permute-start = (bf16[1536,256]{1,0:T(8,128)(2,1)S(1)}, bf16[1536,256]{1,0:T(8,128)(2,1)}, u32[]{:S(2)}, u32[]{:S(2)}) collective-permute-start(bf16[1536,256]{1,0:T(8,128)(2,1)S(1)} %copy-done.42), channel_id=1, source_target_pairs={{0,4},{4,0},{8,12},{12,8},{16,20},{20,16},{24,28},{28,24},{1,5},{5... | collective-permute-start | bytes 2359304 | tf_op jit(solution)/shard_map/ppermute | solution.py:20
  262.3 35.4 %collective-permute-start.1 = (bf16[1536,512]{1,0:T(8,128)(2,1)}, bf16[1536,512]{1,0:T(8,128)(2,1)}, u32[]{:S(2)}, u32[]{:S(2)}) collective-permute-start(bf16[1536,512]{1,0:T(8,128)(2,1)} %maximum_select_fusion.2), channel_id=1, source_target_pairs={{0,8},{4,12},{8,0},{12,4},{16,24},{20,28},{24,16},{28,20},{1,9},{5... | collective-permute-start | bytes 4718600 | tf_op jit(solution)/shard_map/ppermute | solution.py:20
  262.4 577.7 %all-reduce.6.cloned.1.call-start = ((), (), s32[]{:S(2)}) async-start(), calls=%async_computation.19 | async-start | bytes 16777216 | tf_op jit(solution)/shard_map/psum | solution.py:164
  302.8 96.0 %copy-start.49 = (f32[2048]{0:T(1024)S(1)}, f32[2048]{0:T(1024)}, u32[]{:S(2)}) copy-start(f32[2048]{0:T(1024)} %param.21) | copy-start | bytes 24580
  302.8 325.1 %collective-permute-start.2 = (bf16[1536,1024]{1,0:T(8,128)(2,1)}, bf16[1536,1024]{1,0:T(8,128)(2,1)}, u32[]{:S(2)}, u32[]{:S(2)}) collective-permute-start(bf16[1536,1024]{1,0:T(8,128)(2,1)} %maximum_select_fusion.1), channel_id=1, source_target_pairs={{0,16},{4,20},{8,24},{12,28},{16,0},{20,4},{24,8},{28,12},{1,17},{... | collective-permute-start | bytes 9437192 | tf_op jit(solution)/shard_map/ppermute | solution.py:20
  395.5 3.3 copy-start
  668.2 9.9 copy-start.59
  668.2 9.9 copy-start.61
  687.0 321.7 %reduce-scatter.18.cloned.1.call-start = ((), (), s32[]{:S(2)}) async-start(), calls=%async_computation.23 | async-start | bytes 1179648 | tf_op jit(solution)/shard_map/reduce_scatter | solution.py:235
  840.0 8.2 copy-start.3
  840.0 9.4 copy-start.18
  854.1 3.3 copy-start.1
  875.0 6.2 copy-start.20
  883.2 4.8 copy-start.44
  887.9 5.9 copy-start.15
  887.9 131.4 %reduce-scatter.16.cloned.1.call-start = ((), (), s32[]{:S(2)}) async-start(), calls=%async_computation.22 | async-start | bytes 1179648 | tf_op jit(solution)/shard_map/reduce_scatter | solution.py:232
  896.6 2.3 copy-start.21
  896.6 2.9 copy-start.53
  897.9 2.7 copy-start.23
  900.6 2.4 copy-start.62
  903.0 162.2 %reduce-scatter.10.cloned.1.call-start = ((), (), s32[]{:S(2)}) async-start(), calls=%async_computation.17 | async-start | bytes 5242880 | tf_op jit(solution)/shard_map/reduce_scatter | solution.py:150
  916.5 3.9 copy-start.17
  916.5 221.5 %reduce-scatter.14.cloned.1.call-start = ((), (), s32[]{:S(2)}) async-start(), calls=%async_computation.21 | async-start | bytes 2359296 | tf_op jit(solution)/shard_map/reduce_scatter | solution.py:229
  924.6 7.7 copy-start.28
  927.6 4.7 copy-start.7
  946.3 5.2 copy-start.36
  946.3 5.2 copy-start.46
  946.3 5.2 copy-start.50
  953.8 3.9 copy-start.32
  957.7 7.6 copy-start.34
  957.7 7.6 copy-start.37
  957.7 251.7 %reduce-scatter.20.cloned.1.call-start = ((), (), s32[]{:S(2)}) async-start(), calls=%async_computation.24 | async-start | bytes 2359296 | tf_op jit(solution)/shard_map/reduce_scatter | solution.py:238
  965.0 290.2 %reduce-scatter.12.cloned.1.call-start = ((), (), s32[]{:S(2)}) async-start(), calls=%async_computation.20 | async-start | bytes 5242880 | tf_op jit(solution)/shard_map/reduce_scatter | solution.py:225
  966.9 2.4 copy-start.35
  966.9 2.4 copy-start.38
  972.7 404.0 %reduce-scatter.22.cloned.1.call-start = ((), (), s32[]{:S(2)}) async-start(), calls=%async_computation.25 | async-start | bytes 7077888 | tf_op jit(solution)/shard_map/reduce_scatter | solution.py:177
  984.4 513.0 %reduce-scatter.24.cloned.1.call-start = ((), (), s32[]{:S(2)}) async-start(), calls=%async_computation.26 | async-start | bytes 7077888 | tf_op jit(solution)/shard_map/reduce_scatter | solution.py:180
  996.3 623.5 %reduce-scatter.26.cloned.1.call-start = ((), (), s32[]{:S(2)}) async-start(), calls=%async_computation.27 | async-start | bytes 7077888 | tf_op jit(solution)/shard_map/reduce_scatter | solution.py:183
  1007.7 247.5 %copy-start.11 = (bf16[1024,512]{1,0:T(8,128)(2,1)S(1)}, bf16[1024,512]{1,0:T(8,128)(2,1)}, u32[]{:S(2)}) copy-start(bf16[1024,512]{1,0:T(8,128)(2,1)} %param.13) | copy-start | bytes 3145732
  1007.7 247.5 %copy-start.52 = (f32[1024]{0:T(1024)S(1)}, f32[1024]{0:T(1024)}, u32[]{:S(2)}) copy-start(f32[1024]{0:T(1024)} %copy-done.51) | copy-start | bytes 12292
  1211.2 411.0 %copy-start.54 = (f32[1024]{0:T(1024)S(1)}, f32[1024]{0:T(1024)}, u32[]{:S(2)}) copy-start(f32[1024]{0:T(1024)} %get-tuple-element.48) | copy-start | bytes 12292
  1255.2 367.0 %copy-start.25 = (bf16[1024,512]{1,0:T(8,128)(2,1)S(1)}, bf16[1024,512]{1,0:T(8,128)(2,1)}, u32[]{:S(2)}) copy-start(bf16[1024,512]{1,0:T(8,128)(2,1)} %reduce-scatter.12.cloned.1.call-done) | copy-start | bytes 3145732
  (21 other events, 35.1 us)
Sparse Core Ops, SparseCore 0:
  9.6 37.1 all-gather.8
  48.9 49.0 all-gather.14
  100.1 38.7 all-gather.12
  141.0 38.9 all-gather.10
  181.9 49.0 all-gather.16
  238.7 151.0 all-reduce.3
  392.0 124.2 all-gather.18
  518.5 97.7 all-gather.20
  617.8 32.6 all-gather.22
  687.1 152.8 all-reduce.5
  888.0 64.3 reduce-scatter.17
  956.2 63.0 reduce-scatter.15
  1021.9 43.3 reduce-scatter.9
  1069.2 68.7 reduce-scatter.13
  1141.3 68.0 reduce-scatter.19
  1211.8 43.3 reduce-scatter.11
  1258.6 118.0 reduce-scatter.21
  1380.1 117.2 reduce-scatter.23
  1501.0 118.7 reduce-scatter.25
